TPU v7x, 32 devices: a whole 2x2x4 slice. The times are simulated.
32 devices in a mesh: row: 8 (over y, x, core), col: 4 (over z).
Axes of the slice: x: 2, y: 2, z: 4, core: 2. Of those that a mesh axis runs over, the one named last changes fastest.
Arguments:
- a_panels: bfloat16 [16384, 1024], P('row', 'col'), may hold values from -6 to 6
- a_mask: int32 [128, 8], P('row', 'col'), may hold values 0 or 1
- b_panels: bfloat16 [1024, 4096], P('row', 'col'), may hold values from -0.1875 to 0.1875
- b_mask: int32 [8, 32], P('row', 'col'), may hold values 0 or 1
- owner_map: int32 [128, 1], P('row'), may hold values from 0 to 7; in each aligned block of 16 rows (0 to 15, 16 to 31, ...) at most 2 rows name the same one
Outputs:
- owned: bfloat16 [16384, 4096], P('row', 'col')
Inputs may be any that keep to these rules, and one draw needn't show every extreme that they name: `owner_map`: within each aligned block of 16 tile rows (the tile rows of one grid row) no owner is named more than 2 times, a bound that some block reaches.
All inputs are finite; a program needn't handle non-finite values. No bound on the sum of `a_mask` or of `b_mask` on one device may be relied on, other than what follows from the above.
Results may differ from a plain program's by a relative error of at most 0.001.
Values may be sent and summed in bfloat16 or wider, within the bound.
No kernel may reach another device: no remote copies, remote signals or barrier semaphores. Data moves between devices by JAX's collectives and lax.ppermute only.
A program may use at most 128 MiB of HBM per device.

v0:
```python
import jax
import jax.numpy as jnp
from jax import lax
from jax.sharding import PartitionSpec as P

SLOTS = 2


def from_behind(value, axis, steps):
    count = lax.axis_size(axis)
    pairs = [(source, (source + steps) % count) for source in range(count)]
    return lax.ppermute(value, axis, pairs)


def masked_a(panel, mask):
    tile_rows = mask.shape[0]
    inner = mask.shape[1]
    tiles = panel.reshape(tile_rows, panel.shape[0] // tile_rows, inner, panel.shape[1] // inner)
    return (tiles * mask.astype(jnp.bfloat16)[:, None, :, None]).reshape(panel.shape)


def masked_b(panel, mask):
    inner = mask.shape[0]
    tile_cols = mask.shape[1]
    tiles = panel.reshape(inner, panel.shape[0] // inner, tile_cols, panel.shape[1] // tile_cols)
    return (tiles * mask.astype(jnp.bfloat16)[:, None, :, None]).reshape(panel.shape)


def product(panel_a, mask_a, panel_b, mask_b):
    return jnp.dot(
        masked_a(panel_a, mask_a), masked_b(panel_b, mask_b), preferred_element_type=jnp.float32
    )


def on_device(a_panels, a_mask, b_panels, b_mask, owner_map):
    tile = b_panels.shape[0]
    depth = lax.axis_size("col")
    grid_rows = lax.axis_size("row")
    fold = grid_rows // depth
    row_id = lax.axis_index("row")
    col_id = lax.axis_index("col")
    panel_b, mask_b = (b_panels, b_mask)
    target = fold * col_id
    for bit in range((grid_rows - 1).bit_length()):
        moved_b, moved_bm = from_behind((panel_b, mask_b), "row", -(1 << bit))
        take = target >> bit & 1 == 1
        panel_b = jnp.where(take, moved_b, panel_b)
        mask_b = jnp.where(take, moved_bm, mask_b)
    total = jnp.zeros((a_panels.shape[0], b_panels.shape[1]), jnp.float32)
    panel_a, mask_a = (a_panels, a_mask)
    whole_shift = row_id // fold
    remain = row_id % fold
    for bit in range((depth - 1).bit_length()):
        moved_a, moved_am = from_behind((panel_a, mask_a), "col", -(1 << bit))
        take = whole_shift >> bit & 1 == 1
        panel_a = jnp.where(take, moved_a, panel_a)
        mask_a = jnp.where(take, moved_am, mask_a)
    after_a, after_am = from_behind((panel_a, mask_a), "col", -1)
    joined = jnp.concatenate([panel_a, after_a], axis=1)
    joined_m = jnp.concatenate([mask_a, after_am], axis=1)
    panel_a = lax.dynamic_slice_in_dim(joined, remain * tile, fold * tile, 1)
    mask_a = lax.dynamic_slice_in_dim(joined_m, remain, fold, 1)

    def advance(step, carry):
        acc, cur_a, cur_am, cur_b, cur_bm = carry
        acc = acc + product(cur_a[:, :tile], cur_am[:, :1], cur_b, cur_bm)
        head_a, head_m = from_behind((cur_a[:, :tile], cur_am[:, :1]), "col", -1)
        cur_a = jnp.concatenate([cur_a[:, tile:], head_a], axis=1)
        cur_am = jnp.concatenate([cur_am[:, 1:], head_m], axis=1)
        cur_b, cur_bm = from_behind((cur_b, cur_bm), "row", -1)
        return (acc, cur_a, cur_am, cur_b, cur_bm)

    total, panel_a, mask_a, panel_b, mask_b = lax.fori_loop(
        0, grid_rows - 1, advance, (total, panel_a, mask_a, panel_b, mask_b)
    )
    total = total + product(panel_a[:, :tile], mask_a[:, :1], panel_b, mask_b)
    result = total.astype(jnp.bfloat16)
    owners = owner_map[:, 0]
    tile_rows = owners.shape[0]
    same = owners[:, None] == owners[None, :]
    earlier = (
        jnp.arange(tile_rows, dtype=jnp.int32)[None, :]
        < jnp.arange(tile_rows, dtype=jnp.int32)[:, None]
    )
    rank = jnp.sum(jnp.where(same & earlier, 1, 0).astype(jnp.int32), axis=1)
    slot_id = owners * SLOTS + rank
    select = (jnp.arange(grid_rows * SLOTS, dtype=jnp.int32)[:, None] == slot_id[None, :]).astype(
        jnp.bfloat16
    )
    packed = jnp.dot(
        select, result.reshape(tile_rows, -1), preferred_element_type=jnp.float32
    ).astype(jnp.bfloat16)
    packed = packed.reshape(grid_rows, SLOTS * tile, result.shape[1])
    arrived = lax.all_to_all(packed, "row", split_axis=0, concat_axis=0, tiled=True)
    return arrived.reshape(-1, result.shape[1])


def solution(mesh):
    placed = (P("row", "col"), P("row", "col"), P("row", "col"), P("row", "col"), P("row", None))
    return jax.shard_map(
        on_device, mesh=mesh, in_specs=placed, out_specs=P("row", "col"), check_vma=False
    )
```

profile of v0, /device:TPU:0, one launch (start us, length us, event | category | flops | bytes accessed | tf_op | source)
XLA Modules:
  0.0 282.8 jit_solution(3299915901711081954)
XLA Ops:
  0.0 5.0 %collective-permute-start.4 = (bf16[2048,256]{1,0:T(8,128)(2,1)}, bf16[2048,256]{1,0:T(8,128)(2,1)S(1)}, u32[]{:S(2)}, u32[]{:S(2)}) collective-permute-start(bf16[2048,256]{1,0:T(8,128)(2,1)} %param.7), channel_id=1, source_target_pairs={{0,3},{1,0},{2,1},{3,2},{4,7},{5,4},{6,5},{7,6},{8,11},{9,8},{10,9... | collective-permute-start | bytes 3145736 | tf_op jit(solution)/shard_map/ppermute | solution.py:12
  9.0 18.8 %collective-permute-done.4 = bf16[2048,256]{1,0:T(8,128)(2,1)S(1)} collective-permute-done((bf16[2048,256]{1,0:T(8,128)(2,1)}, bf16[2048,256]{1,0:T(8,128)(2,1)S(1)}, u32[]{:S(2)}, u32[]{:S(2)}) %collective-permute-start.4) | collective-permute-done | bytes 1048608 | tf_op jit(solution)/shard_map/ppermute | solution.py:12
  40.7 35.9 %collective-permute-done.5 = bf16[2048,256]{1,0:T(8,128)(2,1)S(1)} collective-permute-done((bf16[2048,256]{1,0:T(8,128)(2,1)S(1)}, bf16[2048,256]{1,0:T(8,128)(2,1)S(1)}, u32[]{:S(2)}, u32[]{:S(2)}) %collective-permute-start.5) | collective-permute-done | bytes 1048608 | tf_op jit(solution)/shard_map/ppermute | solution.py:12
  80.8 20.9 %collective-permute-done.9 = s32[16,2]{0,1:T(2,128)S(1)} collective-permute-done((s32[16,2]{0,1:T(2,128)S(1)}, s32[16,2]{0,1:T(2,128)S(1)}, u32[]{:S(2)}, u32[]{:S(2)}) %collective-permute-start.9) | collective-permute-done | bytes 160 | tf_op jit(solution)/shard_map/ppermute | solution.py:12
  102.2 96.9 %while.19 = (s32[]{:T(128)}, f32[2048,1024]{1,0:T(8,128)}, bf16[2048,256]{1,0:T(8,128)(2,1)S(1)}, s32[16,2]{0,1:T(2,128)S(1)}, bf16[128,1024]{1,0:T(8,128)(2,1)S...) while((s32[]{:T(128)}, f32[2048,1024]{1,0:T(8,128)}, bf16[2048,256]{1,0:T(8,128)(2,1)S(1)}, ...), condition=%wide.region_2.3_spmd.clone, body=%wide.region_1.2_spmd.clone.sunk | while | flops 543555584 | bytes 25441596 | solution.py:73
  102.2 4.4 %collective-permute-start = (bf16[2048,128]{1,0:T(8,128)(2,1)S(1)}, bf16[2048,128]{1,0:T(8,128)(2,1)S(1)}, u32[]{:S(2)}, u32[]{:S(2)}) collective-permute-start(bf16[2048,128]{1,0:T(8,128)(2,1)S(1)} %get-tuple-element.127), channel_id=1, source_target_pairs={{0,3},{1,0},{2,1},{3,2},{4,7},{5,4},{6,5},{7,6},{8,11},{9,8},{10,9... | collective-permute-start | bytes 1572872 | tf_op jit(solution)/shard_map/while/body/eval_jaxpr/ppermute | solution.py:12
  108.2 4.5 %select_add_fusion.2 = f32[2048,1024]{1,0:T(8,128)} fusion(f32[2048,1024]{1,0:T(8,128)} %get-tuple-element.140, pred[]{:T(512)S(6)} %compare.6, bf16[128,1024]{1,0:T(8,128)(2,1)S(1)} %copy.16, bf16[2048]{0:T(1024)(128)(2,1)S(1)} %broadcast_bitcast_fusion.6, bf16[1024]{0:T(1024)(128)(2,1)S(1)} %broadcast_bitcast_fusion.7, ...), kind=kOutput, calls=%fused_computation.clone.1 | convolution fusion | flops 541458432 | bytes 17569792 | tf_op jit(solution)/shard_map/while/body/eval_jaxpr/dot_general | solution.py:30
  112.8 4.3 %collective-permute-done.1 = s32[16,1]{0,1:T(1,128)S(1)} collective-permute-done((s32[16,1]{0,1:T(1,128)S(1)}, s32[16,1]{0,1:T(1,128)S(1)}, u32[]{:S(2)}, u32[]{:S(2)}) %collective-permute-start.1) | collective-permute-done | bytes 96 | tf_op jit(solution)/shard_map/while/body/eval_jaxpr/ppermute | solution.py:12
  117.4 4.4 %collective-permute-start = (bf16[2048,128]{1,0:T(8,128)(2,1)S(1)}, bf16[2048,128]{1,0:T(8,128)(2,1)S(1)}, u32[]{:S(2)}, u32[]{:S(2)}) collective-permute-start(bf16[2048,128]{1,0:T(8,128)(2,1)S(1)} %get-tuple-element.127), channel_id=1, source_target_pairs={{0,3},{1,0},{2,1},{3,2},{4,7},{5,4},{6,5},{7,6},{8,11},{9,8},{10,9... | collective-permute-start | bytes 1572872 | tf_op jit(solution)/shard_map/while/body/eval_jaxpr/ppermute | solution.py:12
  123.3 7.9 %select_add_fusion.2 = f32[2048,1024]{1,0:T(8,128)} fusion(f32[2048,1024]{1,0:T(8,128)} %get-tuple-element.140, pred[]{:T(512)S(6)} %compare.6, bf16[128,1024]{1,0:T(8,128)(2,1)S(1)} %copy.16, bf16[2048]{0:T(1024)(128)(2,1)S(1)} %broadcast_bitcast_fusion.6, bf16[1024]{0:T(1024)(128)(2,1)S(1)} %broadcast_bitcast_fusion.7, ...), kind=kOutput, calls=%fused_computation.clone.1 | convolution fusion | flops 541458432 | bytes 17569792 | tf_op jit(solution)/shard_map/while/body/eval_jaxpr/dot_general | solution.py:30
  131.5 4.3 %collective-permute-start = (bf16[2048,128]{1,0:T(8,128)(2,1)S(1)}, bf16[2048,128]{1,0:T(8,128)(2,1)S(1)}, u32[]{:S(2)}, u32[]{:S(2)}) collective-permute-start(bf16[2048,128]{1,0:T(8,128)(2,1)S(1)} %get-tuple-element.127), channel_id=1, source_target_pairs={{0,3},{1,0},{2,1},{3,2},{4,7},{5,4},{6,5},{7,6},{8,11},{9,8},{10,9... | collective-permute-start | bytes 1572872 | tf_op jit(solution)/shard_map/while/body/eval_jaxpr/ppermute | solution.py:12
  137.5 7.9 %select_add_fusion.2 = f32[2048,1024]{1,0:T(8,128)} fusion(f32[2048,1024]{1,0:T(8,128)} %get-tuple-element.140, pred[]{:T(512)S(6)} %compare.6, bf16[128,1024]{1,0:T(8,128)(2,1)S(1)} %copy.16, bf16[2048]{0:T(1024)(128)(2,1)S(1)} %broadcast_bitcast_fusion.6, bf16[1024]{0:T(1024)(128)(2,1)S(1)} %broadcast_bitcast_fusion.7, ...), kind=kOutput, calls=%fused_computation.clone.1 | convolution fusion | flops 541458432 | bytes 17569792 | tf_op jit(solution)/shard_map/while/body/eval_jaxpr/dot_general | solution.py:30
  145.7 3.3 %collective-permute-start = (bf16[2048,128]{1,0:T(8,128)(2,1)S(1)}, bf16[2048,128]{1,0:T(8,128)(2,1)S(1)}, u32[]{:S(2)}, u32[]{:S(2)}) collective-permute-start(bf16[2048,128]{1,0:T(8,128)(2,1)S(1)} %get-tuple-element.127), channel_id=1, source_target_pairs={{0,3},{1,0},{2,1},{3,2},{4,7},{5,4},{6,5},{7,6},{8,11},{9,8},{10,9... | collective-permute-start | bytes 1572872 | tf_op jit(solution)/shard_map/while/body/eval_jaxpr/ppermute | solution.py:12
  150.6 7.9 %select_add_fusion.2 = f32[2048,1024]{1,0:T(8,128)} fusion(f32[2048,1024]{1,0:T(8,128)} %get-tuple-element.140, pred[]{:T(512)S(6)} %compare.6, bf16[128,1024]{1,0:T(8,128)(2,1)S(1)} %copy.16, bf16[2048]{0:T(1024)(128)(2,1)S(1)} %broadcast_bitcast_fusion.6, bf16[1024]{0:T(1024)(128)(2,1)S(1)} %broadcast_bitcast_fusion.7, ...), kind=kOutput, calls=%fused_computation.clone.1 | convolution fusion | flops 541458432 | bytes 17569792 | tf_op jit(solution)/shard_map/while/body/eval_jaxpr/dot_general | solution.py:30
  163.7 7.9 %select_add_fusion.2 = f32[2048,1024]{1,0:T(8,128)} fusion(f32[2048,1024]{1,0:T(8,128)} %get-tuple-element.140, pred[]{:T(512)S(6)} %compare.6, bf16[128,1024]{1,0:T(8,128)(2,1)S(1)} %copy.16, bf16[2048]{0:T(1024)(128)(2,1)S(1)} %broadcast_bitcast_fusion.6, bf16[1024]{0:T(1024)(128)(2,1)S(1)} %broadcast_bitcast_fusion.7, ...), kind=kOutput, calls=%fused_computation.clone.1 | convolution fusion | flops 541458432 | bytes 17569792 | tf_op jit(solution)/shard_map/while/body/eval_jaxpr/dot_general | solution.py:30
  172.4 3.2 %collective-permute-start = (bf16[2048,128]{1,0:T(8,128)(2,1)S(1)}, bf16[2048,128]{1,0:T(8,128)(2,1)S(1)}, u32[]{:S(2)}, u32[]{:S(2)}) collective-permute-start(bf16[2048,128]{1,0:T(8,128)(2,1)S(1)} %get-tuple-element.127), channel_id=1, source_target_pairs={{0,3},{1,0},{2,1},{3,2},{4,7},{5,4},{6,5},{7,6},{8,11},{9,8},{10,9... | collective-permute-start | bytes 1572872 | tf_op jit(solution)/shard_map/while/body/eval_jaxpr/ppermute | solution.py:12
  177.8 7.9 %select_add_fusion.2 = f32[2048,1024]{1,0:T(8,128)} fusion(f32[2048,1024]{1,0:T(8,128)} %get-tuple-element.140, pred[]{:T(512)S(6)} %compare.6, bf16[128,1024]{1,0:T(8,128)(2,1)S(1)} %copy.16, bf16[2048]{0:T(1024)(128)(2,1)S(1)} %broadcast_bitcast_fusion.6, bf16[1024]{0:T(1024)(128)(2,1)S(1)} %broadcast_bitcast_fusion.7, ...), kind=kOutput, calls=%fused_computation.clone.1 | convolution fusion | flops 541458432 | bytes 17569792 | tf_op jit(solution)/shard_map/while/body/eval_jaxpr/dot_general | solution.py:30
  190.9 7.9 %select_add_fusion.2 = f32[2048,1024]{1,0:T(8,128)} fusion(f32[2048,1024]{1,0:T(8,128)} %get-tuple-element.140, pred[]{:T(512)S(6)} %compare.6, bf16[128,1024]{1,0:T(8,128)(2,1)S(1)} %copy.16, bf16[2048]{0:T(1024)(128)(2,1)S(1)} %broadcast_bitcast_fusion.6, bf16[1024]{0:T(1024)(128)(2,1)S(1)} %broadcast_bitcast_fusion.7, ...), kind=kOutput, calls=%fused_computation.clone.1 | convolution fusion | flops 541458432 | bytes 17569792 | tf_op jit(solution)/shard_map/while/body/eval_jaxpr/dot_general | solution.py:30
  199.2 4.6 %fusion.6 = f32[2048,1024]{1,0:T(8,128)} fusion(bf16[2048,256]{1,0:T(8,128)(2,1)S(1)} %get-tuple-element.42, bf16[128,1024]{1,0:T(8,128)(2,1)S(1)} %get-tuple-element.44, bf16[2048]{0:T(1024)(128)(2,1)S(1)} %broadcast_bitcast_fusion.2, bf16[1024]{0:T(1024)(128)(2,1)S(1)} %broadcast_bitcast_fusion.3), kind=kOutput, calls=%fused_computation.19 | convolution fusion | flops 537264128 | bytes 9181184 | tf_op jit(solution)/shard_map/dot_general | solution.py:30
  203.8 9.3 %add_convert_fusion = bf16[2048,1024]{1,0:T(8,128)(2,1)} fusion(f32[2048,1024]{1,0:T(8,128)} %get-tuple-element.41, f32[2048,1024]{1,0:T(8,128)} %fusion.6), kind=kLoop, calls=%fused_computation.13 | loop fusion | flops 4194304 | bytes 20971520 | tf_op jit(solution)/shard_map/convert_element_type | solution.py:77
  213.1 4.8 %reshape.54 = bf16[16,131072]{1,0:T(8,128)(2,1)} reshape(bf16[2048,1024]{1,0:T(8,128)(2,1)} %add_convert_fusion) | data formatting | bytes 8388608 | tf_op jit(solution)/shard_map/reshape | solution.py:91
  217.9 5.4 %convolution_convert_fusion = bf16[16,131072]{1,0:T(8,128)(2,1)} fusion(bf16[16,131072]{1,0:T(8,128)(2,1)} %reshape.54, s32[16]{0:T(128)S(1)} %multiply_add_fusion), kind=kOutput, calls=%fused_computation.12 | convolution fusion | flops 69206272 | bytes 8388672 | tf_op jit(solution)/shard_map/dot_general | solution.py:90
  223.3 4.8 %reshape.55 = bf16[8,256,1024]{2,1,0:T(8,128)(2,1)} reshape(bf16[16,131072]{1,0:T(8,128)(2,1)} %convolution_convert_fusion) | data formatting | bytes 8388608 | tf_op jit(solution)/shard_map/reshape | solution.py:93
  228.2 52.7 %all_to_all.5 = bf16[8,256,1024]{2,1,0:T(8,128)(2,1)S(1)} all-to-all(bf16[8,256,1024]{2,1,0:T(8,128)(2,1)} %reshape.55), channel_id=1, replica_groups=mesh['row'=8,'col'=4] {'row'}, dimensions={0} | all-to-all | bytes 8388608 | tf_op jit(solution)/shard_map/all_to_all | solution.py:94
  (155 shorter events, 44.1 us)
Async XLA Ops:
  0.0 27.8 %collective-permute-start.4 = (bf16[2048,256]{1,0:T(8,128)(2,1)}, bf16[2048,256]{1,0:T(8,128)(2,1)S(1)}, u32[]{:S(2)}, u32[]{:S(2)}) collective-permute-start(bf16[2048,256]{1,0:T(8,128)(2,1)} %param.7), channel_id=1, source_target_pairs={{0,3},{1,0},{2,1},{3,2},{4,7},{5,4},{6,5},{7,6},{8,11},{9,8},{10,9... | collective-permute-start | bytes 3145736 | tf_op jit(solution)/shard_map/ppermute | solution.py:12
  5.0 31.9 %collective-permute-start.7 = (s32[16,2]{0,1:T(2,128)}, s32[16,2]{0,1:T(2,128)S(1)}, u32[]{:S(2)}, u32[]{:S(2)}) collective-permute-start(s32[16,2]{0,1:T(2,128)} %param.8), channel_id=1, source_target_pairs={{0,3},{1,0},{2,1},{3,2},{4,7},{5,4},{6,5},{7,6},{8,11},{9,8},{10,9... | collective-permute-start | bytes 392 | tf_op jit(solution)/shard_map/ppermute | solution.py:12
  5.5 33.7 %collective-permute-start.10 = (bf16[128,1024]{1,0:T(8,128)(2,1)}, bf16[128,1024]{1,0:T(8,128)(2,1)S(1)}, u32[]{:S(2)}, u32[]{:S(2)}) collective-permute-start(bf16[128,1024]{1,0:T(8,128)(2,1)} %param.9), channel_id=1, source_target_pairs={{0,28},{4,0},{8,4},{12,8},{16,12},{20,16},{24,20},{28,24},{1,29},{... | collective-permute-start | bytes 786440 | tf_op jit(solution)/shard_map/ppermute | solution.py:12
  6.8 24.4 %collective-permute-start.13 = (s32[1,8]{1,0:T(1,128)}, s32[1,8]{1,0:T(1,128)S(1)}, u32[]{:S(2)}, u32[]{:S(2)}) collective-permute-start(s32[1,8]{1,0:T(1,128)} %param.10), channel_id=1, source_target_pairs={{0,28},{4,0},{8,4},{12,8},{16,12},{20,16},{24,20},{28,24},{1,29},{... | collective-permute-start | bytes 104 | tf_op jit(solution)/shard_map/ppermute | solution.py:12
  29.1 47.5 %collective-permute-start.5 = (bf16[2048,256]{1,0:T(8,128)(2,1)S(1)}, bf16[2048,256]{1,0:T(8,128)(2,1)S(1)}, u32[]{:S(2)}, u32[]{:S(2)}) collective-permute-start(bf16[2048,256]{1,0:T(8,128)(2,1)S(1)} %broadcast_select_fusion), channel_id=1, source_target_pairs={{0,2},{1,3},{2,0},{3,1},{4,6},{5,7},{6,4},{7,5},{8,10},{9,11},{10,... | collective-permute-start | bytes 3145736 | tf_op jit(solution)/shard_map/ppermute | solution.py:12
  35.4 45.3 %collective-permute-start.15 = (s32[1,8]{1,0:T(1,128)S(1)}, s32[1,8]{1,0:T(1,128)S(1)}, u32[]{:S(2)}, u32[]{:S(2)}) collective-permute-start(s32[1,8]{1,0:T(1,128)S(1)} %broadcast_select_fusion.6), channel_id=1, source_target_pairs={{0,16},{4,20},{8,24},{12,28},{16,0},{20,4},{24,8},{28,12},{1,17},{... | collective-permute-start | bytes 104 | tf_op jit(solution)/shard_map/ppermute | solution.py:12
  37.6 41.4 %collective-permute-start.8 = (s32[16,2]{0,1:T(2,128)S(1)}, s32[16,2]{0,1:T(2,128)S(1)}, u32[]{:S(2)}, u32[]{:S(2)}) collective-permute-start(s32[16,2]{0,1:T(2,128)S(1)} %broadcast_select_fusion.8), channel_id=1, source_target_pairs={{0,2},{1,3},{2,0},{3,1},{4,6},{5,7},{6,4},{7,5},{8,10},{9,11},{10,... | collective-permute-start | bytes 392 | tf_op jit(solution)/shard_map/ppermute | solution.py:12
  40.2 39.0 %collective-permute-start.11 = (bf16[128,1024]{1,0:T(8,128)(2,1)S(1)}, bf16[128,1024]{1,0:T(8,128)(2,1)S(1)}, u32[]{:S(2)}, u32[]{:S(2)}) collective-permute-start(bf16[128,1024]{1,0:T(8,128)(2,1)S(1)} %broadcast_select_fusion.2), channel_id=1, source_target_pairs={{0,24},{4,28},{8,0},{12,4},{16,8},{20,12},{24,16},{28,20},{1,25},{... | collective-permute-start | bytes 786440 | tf_op jit(solution)/shard_map/ppermute | solution.py:12
  76.7 25.0 %collective-permute-start.6 = (bf16[2048,256]{1,0:T(8,128)(2,1)S(1)}, bf16[2048,256]{1,0:T(8,128)(2,1)S(1)}, u32[]{:S(2)}, u32[]{:S(2)}) collective-permute-start(bf16[2048,256]{1,0:T(8,128)(2,1)S(1)} %broadcast_select_fusion.1), channel_id=1, source_target_pairs={{0,3},{1,0},{2,1},{3,2},{4,7},{5,4},{6,5},{7,6},{8,11},{9,8},{10,9... | collective-permute-start | bytes 3145736 | tf_op jit(solution)/shard_map/ppermute | solution.py:12
  79.1 22.6 %collective-permute-start.9 = (s32[16,2]{0,1:T(2,128)S(1)}, s32[16,2]{0,1:T(2,128)S(1)}, u32[]{:S(2)}, u32[]{:S(2)}) collective-permute-start(s32[16,2]{0,1:T(2,128)S(1)} %broadcast_select_fusion.9), channel_id=1, source_target_pairs={{0,3},{1,0},{2,1},{3,2},{4,7},{5,4},{6,5},{7,6},{8,11},{9,8},{10,9... | collective-permute-start | bytes 392 | tf_op jit(solution)/shard_map/ppermute | solution.py:12
  79.2 22.5 %collective-permute-start.12 = (bf16[128,1024]{1,0:T(8,128)(2,1)S(1)}, bf16[128,1024]{1,0:T(8,128)(2,1)S(1)}, u32[]{:S(2)}, u32[]{:S(2)}) collective-permute-start(bf16[128,1024]{1,0:T(8,128)(2,1)S(1)} %broadcast_select_fusion.3), channel_id=1, source_target_pairs={{0,16},{4,20},{8,24},{12,28},{16,0},{20,4},{24,8},{28,12},{1,17},{... | collective-permute-start | bytes 786440 | tf_op jit(solution)/shard_map/ppermute | solution.py:12
  102.2 14.9 %collective-permute-start = (bf16[2048,128]{1,0:T(8,128)(2,1)S(1)}, bf16[2048,128]{1,0:T(8,128)(2,1)S(1)}, u32[]{:S(2)}, u32[]{:S(2)}) collective-permute-start(bf16[2048,128]{1,0:T(8,128)(2,1)S(1)} %get-tuple-element.127), channel_id=1, source_target_pairs={{0,3},{1,0},{2,1},{3,2},{4,7},{5,4},{6,5},{7,6},{8,11},{9,8},{10,9... | collective-permute-start | bytes 1572872 | tf_op jit(solution)/shard_map/while/body/eval_jaxpr/ppermute | solution.py:12
  106.6 10.5 %collective-permute-start.1 = (s32[16,1]{0,1:T(1,128)S(1)}, s32[16,1]{0,1:T(1,128)S(1)}, u32[]{:S(2)}, u32[]{:S(2)}) collective-permute-start(s32[16,1]{0,1:T(1,128)S(1)} %get-tuple-element.129), channel_id=1, source_target_pairs={{0,3},{1,0},{2,1},{3,2},{4,7},{5,4},{6,5},{7,6},{8,11},{9,8},{10,9... | collective-permute-start | bytes 200 | tf_op jit(solution)/shard_map/while/body/eval_jaxpr/ppermute | solution.py:12
  106.7 10.6 %collective-permute-start.2 = (bf16[128,1024]{1,0:T(8,128)(2,1)S(1)}, bf16[128,1024]{1,0:T(8,128)(2,1)S(1)}, u32[]{:S(2)}, u32[]{:S(2)}) collective-permute-start(bf16[128,1024]{1,0:T(8,128)(2,1)S(1)} %copy.16), channel_id=1, source_target_pairs={{0,28},{4,0},{8,4},{12,8},{16,12},{20,16},{24,20},{28,24},{1,29},{... | collective-permute-start | bytes 786440 | tf_op jit(solution)/shard_map/while/body/eval_jaxpr/ppermute | solution.py:12
  106.8 10.5 %collective-permute-start.3 = (s32[1,8]{1,0:T(1,128)S(1)}, s32[1,8]{1,0:T(1,128)S(1)}, u32[]{:S(2)}, u32[]{:S(2)}) collective-permute-start(s32[1,8]{1,0:T(1,128)S(1)} %copy.17), channel_id=1, source_target_pairs={{0,28},{4,0},{8,4},{12,8},{16,12},{20,16},{24,20},{28,24},{1,29},{... | collective-permute-start | bytes 104 | tf_op jit(solution)/shard_map/while/body/eval_jaxpr/ppermute | solution.py:12
  117.4 13.9 %collective-permute-start = (bf16[2048,128]{1,0:T(8,128)(2,1)S(1)}, bf16[2048,128]{1,0:T(8,128)(2,1)S(1)}, u32[]{:S(2)}, u32[]{:S(2)}) collective-permute-start(bf16[2048,128]{1,0:T(8,128)(2,1)S(1)} %get-tuple-element.127), channel_id=1, source_target_pairs={{0,3},{1,0},{2,1},{3,2},{4,7},{5,4},{6,5},{7,6},{8,11},{9,8},{10,9... | collective-permute-start | bytes 1572872 | tf_op jit(solution)/shard_map/while/body/eval_jaxpr/ppermute | solution.py:12
  131.5 13.9 %collective-permute-start = (bf16[2048,128]{1,0:T(8,128)(2,1)S(1)}, bf16[2048,128]{1,0:T(8,128)(2,1)S(1)}, u32[]{:S(2)}, u32[]{:S(2)}) collective-permute-start(bf16[2048,128]{1,0:T(8,128)(2,1)S(1)} %get-tuple-element.127), channel_id=1, source_target_pairs={{0,3},{1,0},{2,1},{3,2},{4,7},{5,4},{6,5},{7,6},{8,11},{9,8},{10,9... | collective-permute-start | bytes 1572872 | tf_op jit(solution)/shard_map/while/body/eval_jaxpr/ppermute | solution.py:12
  145.7 13.4 %collective-permute-start = (bf16[2048,128]{1,0:T(8,128)(2,1)S(1)}, bf16[2048,128]{1,0:T(8,128)(2,1)S(1)}, u32[]{:S(2)}, u32[]{:S(2)}) collective-permute-start(bf16[2048,128]{1,0:T(8,128)(2,1)S(1)} %get-tuple-element.127), channel_id=1, source_target_pairs={{0,3},{1,0},{2,1},{3,2},{4,7},{5,4},{6,5},{7,6},{8,11},{9,8},{10,9... | collective-permute-start | bytes 1572872 | tf_op jit(solution)/shard_map/while/body/eval_jaxpr/ppermute | solution.py:12
  159.3 12.9 %collective-permute-start = (bf16[2048,128]{1,0:T(8,128)(2,1)S(1)}, bf16[2048,128]{1,0:T(8,128)(2,1)S(1)}, u32[]{:S(2)}, u32[]{:S(2)}) collective-permute-start(bf16[2048,128]{1,0:T(8,128)(2,1)S(1)} %get-tuple-element.127), channel_id=1, source_target_pairs={{0,3},{1,0},{2,1},{3,2},{4,7},{5,4},{6,5},{7,6},{8,11},{9,8},{10,9... | collective-permute-start | bytes 1572872 | tf_op jit(solution)/shard_map/while/body/eval_jaxpr/ppermute | solution.py:12
  161.5 10.7 %collective-permute-start.1 = (s32[16,1]{0,1:T(1,128)S(1)}, s32[16,1]{0,1:T(1,128)S(1)}, u32[]{:S(2)}, u32[]{:S(2)}) collective-permute-start(s32[16,1]{0,1:T(1,128)S(1)} %get-tuple-element.129), channel_id=1, source_target_pairs={{0,3},{1,0},{2,1},{3,2},{4,7},{5,4},{6,5},{7,6},{8,11},{9,8},{10,9... | collective-permute-start | bytes 200 | tf_op jit(solution)/shard_map/while/body/eval_jaxpr/ppermute | solution.py:12
  161.6 10.7 %collective-permute-start.2 = (bf16[128,1024]{1,0:T(8,128)(2,1)S(1)}, bf16[128,1024]{1,0:T(8,128)(2,1)S(1)}, u32[]{:S(2)}, u32[]{:S(2)}) collective-permute-start(bf16[128,1024]{1,0:T(8,128)(2,1)S(1)} %copy.16), channel_id=1, source_target_pairs={{0,28},{4,0},{8,4},{12,8},{16,12},{20,16},{24,20},{28,24},{1,29},{... | collective-permute-start | bytes 786440 | tf_op jit(solution)/shard_map/while/body/eval_jaxpr/ppermute | solution.py:12
  161.7 10.6 %collective-permute-start.3 = (s32[1,8]{1,0:T(1,128)S(1)}, s32[1,8]{1,0:T(1,128)S(1)}, u32[]{:S(2)}, u32[]{:S(2)}) collective-permute-start(s32[1,8]{1,0:T(1,128)S(1)} %copy.17), channel_id=1, source_target_pairs={{0,28},{4,0},{8,4},{12,8},{16,12},{20,16},{24,20},{28,24},{1,29},{... | collective-permute-start | bytes 104 | tf_op jit(solution)/shard_map/while/body/eval_jaxpr/ppermute | solution.py:12
  172.4 13.3 %collective-permute-start = (bf16[2048,128]{1,0:T(8,128)(2,1)S(1)}, bf16[2048,128]{1,0:T(8,128)(2,1)S(1)}, u32[]{:S(2)}, u32[]{:S(2)}) collective-permute-start(bf16[2048,128]{1,0:T(8,128)(2,1)S(1)} %get-tuple-element.127), channel_id=1, source_target_pairs={{0,3},{1,0},{2,1},{3,2},{4,7},{5,4},{6,5},{7,6},{8,11},{9,8},{10,9... | collective-permute-start | bytes 1572872 | tf_op jit(solution)/shard_map/while/body/eval_jaxpr/ppermute | solution.py:12
  186.0 12.9 %collective-permute-start = (bf16[2048,128]{1,0:T(8,128)(2,1)S(1)}, bf16[2048,128]{1,0:T(8,128)(2,1)S(1)}, u32[]{:S(2)}, u32[]{:S(2)}) collective-permute-start(bf16[2048,128]{1,0:T(8,128)(2,1)S(1)} %get-tuple-element.127), channel_id=1, source_target_pairs={{0,3},{1,0},{2,1},{3,2},{4,7},{5,4},{6,5},{7,6},{8,11},{9,8},{10,9... | collective-permute-start | bytes 1572872 | tf_op jit(solution)/shard_map/while/body/eval_jaxpr/ppermute | solution.py:12
  (16 other events, 151.0 us)
where the time goes:
time: 283 us
  waiting for transfers between devices  83.4 us (29%)
  matrix products  62.1 us (22%)
  starting transfers between devices  54.5 us (19%)
  blocking collectives  52.7 us (19%)
  other arithmetic  16 us (6%)
  local copies, waits for them, and re-layouts  13.5 us (5%)
    ppermute x40, waiting for transfers between devices, from_behind(): return lax.ppermute(value, axis, pairs)  83.4 us
    dot_general x8, matrix products, product(): jnp.dot(masked_a(panel_a, mask_a), masked_b(panel_b, mask_b), preferred_e...  56.6 us
    ppermute x40, starting transfers between devices, from_behind(): return lax.ppermute(value, axis, pairs)  54.5 us
    all_to_all x1, blocking collectives, on_device(): lax.all_to_all(packed, 'row', split_axis=0, concat_axis=0, tiled=True)  52.7 us
    convert_element_type x1, other arithmetic, on_device(): result = total.astype(jnp.bfloat16)  9.3 us
  transfers between devices with their start and end apart: 40, of which 7 were waited for; matrix products, arithmetic and copies ran while one was open for 21% of the time, Pallas kernels for 0%

commit v1 on v0

--- a/solution.py
+++ b/solution.py
@@ -91,7 +91,21 @@
         select, result.reshape(tile_rows, -1), preferred_element_type=jnp.float32
     ).astype(jnp.bfloat16)
     packed = packed.reshape(grid_rows, SLOTS * tile, result.shape[1])
-    arrived = lax.all_to_all(packed, "row", split_axis=0, concat_axis=0, tiled=True)
+    odd = lax.psum(1, axis_name="row")
+    s_next = lax.axis_index("row")
+    latest, z = (odd, s_next)
+    near = packed.shape[0] // latest
+    left_arr = list(packed.shape)
+    left_arr[0] = near
+    value_now = left_arr[0]
+    left_arr[0] = value_now * latest
+    arrived = jnp.zeros(left_arr, packed.dtype)
+    for m in range(latest):
+        long_array = lax.dynamic_slice_in_dim(packed, (z ^ m) * near, near, axis=0)
+        if m:
+            side_arr = tuple(((tick, tick ^ m) for tick in range(latest)))
+            long_array = lax.ppermute(long_array, axis_name="row", perm=side_arr)
+        arrived = lax.dynamic_update_slice_in_dim(arrived, long_array, (z ^ m) * value_now, axis=0)
     return arrived.reshape(-1, result.shape[1])
 
 

time: 283 us -> 283 us (level)
  blocking collectives: 52.7 us -> 0 us
  waiting for transfers between devices: 83.4 us -> 126 us
  starting transfers between devices: 54.5 us -> 60.4 us
  local copies, waits for them, and re-layouts: 13.5 us -> 16.4 us
    all_to_all x1 -> x0, blocking collectives: 52.7 us -> none  [on_device(): lax.all_to_all(packed, 'row', split_axis=0, concat_axis=0, tiled=True)]
    ppermute x0 -> x7, waiting for transfers between devices: none -> 43.1 us  [on_device(): long_array = lax.ppermute(long_array, axis_name='row', perm=side_arr)]
    ppermute x0 -> x7, starting transfers between devices: none -> 5.94 us  [on_device(): long_array = lax.ppermute(long_array, axis_name='row', perm=side_arr)]
  transfers between devices with their start and end apart: 40 -> 47, of which waited for: 7 -> 10; matrix products, arithmetic and copies ran while one was open for 21% -> 21% of each run, Pallas kernels for 0% -> 0%
where the time goes in v1:
time: 283 us; the launch traced here: 282 us
  waiting for transfers between devices  126 us (45%)
  matrix products  62.3 us (22%)
  starting transfers between devices  60.4 us (21%)
  local copies, waits for them, and re-layouts  16.4 us (6%)
  other arithmetic  16 us (6%)
    ppermute x40, waiting for transfers between devices, from_behind(): return lax.ppermute(value, axis, pairs)  83.3 us
    dot_general x8, matrix products, product(): jnp.dot(masked_a(panel_a, mask_a), masked_b(panel_b, mask_b), preferred_e...  56.9 us
    ppermute x40, starting transfers between devices, from_behind(): return lax.ppermute(value, axis, pairs)  54.5 us
    ppermute x7, waiting for transfers between devices, on_device(): long_array = lax.ppermute(long_array, axis_name='row', perm=side_arr)  43.1 us
    convert_element_type x1, other arithmetic, on_device(): result = total.astype(jnp.bfloat16)  9.3 us
    ppermute x7, starting transfers between devices, on_device(): long_array = lax.ppermute(long_array, axis_name='row', perm=side_arr)  5.94 us
  transfers between devices with their start and end apart: 47, of which 10 were waited for; matrix products, arithmetic and copies ran while one was open for 21% of the time, Pallas kernels for 0%

profile of v1, /device:TPU:0, one launch (start us, length us, event | category | flops | bytes accessed | tf_op | source)
XLA Modules:
  0.0 282.4 jit_solution(15024980332956054278)
XLA Ops:
  0.0 5.0 %collective-permute-start.4 = (bf16[2048,256]{1,0:T(8,128)(2,1)}, bf16[2048,256]{1,0:T(8,128)(2,1)S(1)}, u32[]{:S(2)}, u32[]{:S(2)}) collective-permute-start(bf16[2048,256]{1,0:T(8,128)(2,1)} %param.7), channel_id=1, source_target_pairs={{0,3},{1,0},{2,1},{3,2},{4,7},{5,4},{6,5},{7,6},{8,11},{9,8},{10,9... | collective-permute-start | bytes 3145736 | tf_op jit(solution)/shard_map/ppermute | solution.py:12
  9.0 18.8 %collective-permute-done.4 = bf16[2048,256]{1,0:T(8,128)(2,1)S(1)} collective-permute-done((bf16[2048,256]{1,0:T(8,128)(2,1)}, bf16[2048,256]{1,0:T(8,128)(2,1)S(1)}, u32[]{:S(2)}, u32[]{:S(2)}) %collective-permute-start.4) | collective-permute-done | bytes 1048608 | tf_op jit(solution)/shard_map/ppermute | solution.py:12
  40.7 35.9 %collective-permute-done.5 = bf16[2048,256]{1,0:T(8,128)(2,1)S(1)} collective-permute-done((bf16[2048,256]{1,0:T(8,128)(2,1)S(1)}, bf16[2048,256]{1,0:T(8,128)(2,1)S(1)}, u32[]{:S(2)}, u32[]{:S(2)}) %collective-permute-start.5) | collective-permute-done | bytes 1048608 | tf_op jit(solution)/shard_map/ppermute | solution.py:12
  80.8 20.9 %collective-permute-done.9 = s32[16,2]{0,1:T(2,128)S(1)} collective-permute-done((s32[16,2]{0,1:T(2,128)S(1)}, s32[16,2]{0,1:T(2,128)S(1)}, u32[]{:S(2)}, u32[]{:S(2)}) %collective-permute-start.9) | collective-permute-done | bytes 160 | tf_op jit(solution)/shard_map/ppermute | solution.py:12
  102.2 97.0 %while.19 = (s32[]{:T(128)}, f32[2048,1024]{1,0:T(8,128)}, bf16[2048,256]{1,0:T(8,128)(2,1)S(1)}, s32[16,2]{0,1:T(2,128)S(1)}, bf16[128,1024]{1,0:T(8,128)(2,1)S...) while((s32[]{:T(128)}, f32[2048,1024]{1,0:T(8,128)}, bf16[2048,256]{1,0:T(8,128)(2,1)S(1)}, ...), condition=%wide.region_2.3_spmd.clone, body=%wide.region_1.2_spmd.clone.sunk | while | flops 543555584 | bytes 25441596 | solution.py:73
  102.2 4.4 %collective-permute-start = (bf16[2048,128]{1,0:T(8,128)(2,1)S(1)}, bf16[2048,128]{1,0:T(8,128)(2,1)S(1)}, u32[]{:S(2)}, u32[]{:S(2)}) collective-permute-start(bf16[2048,128]{1,0:T(8,128)(2,1)S(1)} %get-tuple-element.135), channel_id=1, source_target_pairs={{0,3},{1,0},{2,1},{3,2},{4,7},{5,4},{6,5},{7,6},{8,11},{9,8},{10,9... | collective-permute-start | bytes 1572872 | tf_op jit(solution)/shard_map/while/body/eval_jaxpr/ppermute | solution.py:12
  108.2 4.6 %select_add_fusion.2 = f32[2048,1024]{1,0:T(8,128)} fusion(f32[2048,1024]{1,0:T(8,128)} %get-tuple-element.148, pred[]{:T(512)S(6)} %compare.6, bf16[128,1024]{1,0:T(8,128)(2,1)S(1)} %copy.16, bf16[2048]{0:T(1024)(128)(2,1)S(1)} %broadcast_bitcast_fusion.6, bf16[1024]{0:T(1024)(128)(2,1)S(1)} %broadcast_bitcast_fusion.7, ...), kind=kOutput, calls=%fused_computation.clone.1 | convolution fusion | flops 541458432 | bytes 17569792 | tf_op jit(solution)/shard_map/while/body/eval_jaxpr/dot_general | solution.py:30
  112.8 4.3 %collective-permute-done.1 = s32[16,1]{0,1:T(1,128)S(1)} collective-permute-done((s32[16,1]{0,1:T(1,128)S(1)}, s32[16,1]{0,1:T(1,128)S(1)}, u32[]{:S(2)}, u32[]{:S(2)}) %collective-permute-start.1) | collective-permute-done | bytes 96 | tf_op jit(solution)/shard_map/while/body/eval_jaxpr/ppermute | solution.py:12
  117.4 4.4 %collective-permute-start = (bf16[2048,128]{1,0:T(8,128)(2,1)S(1)}, bf16[2048,128]{1,0:T(8,128)(2,1)S(1)}, u32[]{:S(2)}, u32[]{:S(2)}) collective-permute-start(bf16[2048,128]{1,0:T(8,128)(2,1)S(1)} %get-tuple-element.135), channel_id=1, source_target_pairs={{0,3},{1,0},{2,1},{3,2},{4,7},{5,4},{6,5},{7,6},{8,11},{9,8},{10,9... | collective-permute-start | bytes 1572872 | tf_op jit(solution)/shard_map/while/body/eval_jaxpr/ppermute | solution.py:12
  123.3 8.0 %select_add_fusion.2 = f32[2048,1024]{1,0:T(8,128)} fusion(f32[2048,1024]{1,0:T(8,128)} %get-tuple-element.148, pred[]{:T(512)S(6)} %compare.6, bf16[128,1024]{1,0:T(8,128)(2,1)S(1)} %copy.16, bf16[2048]{0:T(1024)(128)(2,1)S(1)} %broadcast_bitcast_fusion.6, bf16[1024]{0:T(1024)(128)(2,1)S(1)} %broadcast_bitcast_fusion.7, ...), kind=kOutput, calls=%fused_computation.clone.1 | convolution fusion | flops 541458432 | bytes 17569792 | tf_op jit(solution)/shard_map/while/body/eval_jaxpr/dot_general | solution.py:30
  131.6 4.2 %collective-permute-start = (bf16[2048,128]{1,0:T(8,128)(2,1)S(1)}, bf16[2048,128]{1,0:T(8,128)(2,1)S(1)}, u32[]{:S(2)}, u32[]{:S(2)}) collective-permute-start(bf16[2048,128]{1,0:T(8,128)(2,1)S(1)} %get-tuple-element.135), channel_id=1, source_target_pairs={{0,3},{1,0},{2,1},{3,2},{4,7},{5,4},{6,5},{7,6},{8,11},{9,8},{10,9... | collective-permute-start | bytes 1572872 | tf_op jit(solution)/shard_map/while/body/eval_jaxpr/ppermute | solution.py:12
  137.5 8.0 %select_add_fusion.2 = f32[2048,1024]{1,0:T(8,128)} fusion(f32[2048,1024]{1,0:T(8,128)} %get-tuple-element.148, pred[]{:T(512)S(6)} %compare.6, bf16[128,1024]{1,0:T(8,128)(2,1)S(1)} %copy.16, bf16[2048]{0:T(1024)(128)(2,1)S(1)} %broadcast_bitcast_fusion.6, bf16[1024]{0:T(1024)(128)(2,1)S(1)} %broadcast_bitcast_fusion.7, ...), kind=kOutput, calls=%fused_computation.clone.1 | convolution fusion | flops 541458432 | bytes 17569792 | tf_op jit(solution)/shard_map/while/body/eval_jaxpr/dot_general | solution.py:30
  150.6 8.0 %select_add_fusion.2 = f32[2048,1024]{1,0:T(8,128)} fusion(f32[2048,1024]{1,0:T(8,128)} %get-tuple-element.148, pred[]{:T(512)S(6)} %compare.6, bf16[128,1024]{1,0:T(8,128)(2,1)S(1)} %copy.16, bf16[2048]{0:T(1024)(128)(2,1)S(1)} %broadcast_bitcast_fusion.6, bf16[1024]{0:T(1024)(128)(2,1)S(1)} %broadcast_bitcast_fusion.7, ...), kind=kOutput, calls=%fused_computation.clone.1 | convolution fusion | flops 541458432 | bytes 17569792 | tf_op jit(solution)/shard_map/while/body/eval_jaxpr/dot_general | solution.py:30
  163.8 8.0 %select_add_fusion.2 = f32[2048,1024]{1,0:T(8,128)} fusion(f32[2048,1024]{1,0:T(8,128)} %get-tuple-element.148, pred[]{:T(512)S(6)} %compare.6, bf16[128,1024]{1,0:T(8,128)(2,1)S(1)} %copy.16, bf16[2048]{0:T(1024)(128)(2,1)S(1)} %broadcast_bitcast_fusion.6, bf16[1024]{0:T(1024)(128)(2,1)S(1)} %broadcast_bitcast_fusion.7, ...), kind=kOutput, calls=%fused_computation.clone.1 | convolution fusion | flops 541458432 | bytes 17569792 | tf_op jit(solution)/shard_map/while/body/eval_jaxpr/dot_general | solution.py:30
  177.9 8.0 %select_add_fusion.2 = f32[2048,1024]{1,0:T(8,128)} fusion(f32[2048,1024]{1,0:T(8,128)} %get-tuple-element.148, pred[]{:T(512)S(6)} %compare.6, bf16[128,1024]{1,0:T(8,128)(2,1)S(1)} %copy.16, bf16[2048]{0:T(1024)(128)(2,1)S(1)} %broadcast_bitcast_fusion.6, bf16[1024]{0:T(1024)(128)(2,1)S(1)} %broadcast_bitcast_fusion.7, ...), kind=kOutput, calls=%fused_computation.clone.1 | convolution fusion | flops 541458432 | bytes 17569792 | tf_op jit(solution)/shard_map/while/body/eval_jaxpr/dot_general | solution.py:30
  191.0 8.0 %select_add_fusion.2 = f32[2048,1024]{1,0:T(8,128)} fusion(f32[2048,1024]{1,0:T(8,128)} %get-tuple-element.148, pred[]{:T(512)S(6)} %compare.6, bf16[128,1024]{1,0:T(8,128)(2,1)S(1)} %copy.16, bf16[2048]{0:T(1024)(128)(2,1)S(1)} %broadcast_bitcast_fusion.6, bf16[1024]{0:T(1024)(128)(2,1)S(1)} %broadcast_bitcast_fusion.7, ...), kind=kOutput, calls=%fused_computation.clone.1 | convolution fusion | flops 541458432 | bytes 17569792 | tf_op jit(solution)/shard_map/while/body/eval_jaxpr/dot_general | solution.py:30
  199.3 4.5 %fusion.6 = f32[2048,1024]{1,0:T(8,128)} fusion(bf16[2048,256]{1,0:T(8,128)(2,1)S(1)} %get-tuple-element.42, bf16[128,1024]{1,0:T(8,128)(2,1)S(1)} %get-tuple-element.44, bf16[2048]{0:T(1024)(128)(2,1)S(1)} %broadcast_bitcast_fusion.2, bf16[1024]{0:T(1024)(128)(2,1)S(1)} %broadcast_bitcast_fusion.3), kind=kOutput, calls=%fused_computation.20 | convolution fusion | flops 537264128 | bytes 9181184 | tf_op jit(solution)/shard_map/dot_general | solution.py:30
  203.9 9.3 %add_convert_fusion = bf16[2048,1024]{1,0:T(8,128)(2,1)} fusion(f32[2048,1024]{1,0:T(8,128)} %get-tuple-element.41, f32[2048,1024]{1,0:T(8,128)} %fusion.6), kind=kLoop, calls=%fused_computation.13 | loop fusion | flops 4194304 | bytes 20971520 | tf_op jit(solution)/shard_map/convert_element_type | solution.py:77
  213.2 4.8 %reshape.54 = bf16[16,131072]{1,0:T(8,128)(2,1)} reshape(bf16[2048,1024]{1,0:T(8,128)(2,1)} %add_convert_fusion) | data formatting | bytes 8388608 | tf_op jit(solution)/shard_map/reshape | solution.py:91
  218.0 5.4 %convolution_convert_fusion = bf16[16,131072]{1,0:T(8,128)(2,1)} fusion(bf16[16,131072]{1,0:T(8,128)(2,1)} %reshape.54, s32[16]{0:T(128)S(1)} %multiply_add_fusion), kind=kOutput, calls=%fused_computation.12 | convolution fusion | flops 69206272 | bytes 8388672 | tf_op jit(solution)/shard_map/dot_general | solution.py:90
  223.4 4.8 %reshape.55 = bf16[8,256,1024]{2,1,0:T(8,128)(2,1)} reshape(bf16[16,131072]{1,0:T(8,128)(2,1)} %convolution_convert_fusion) | data formatting | bytes 8388608 | tf_op jit(solution)/shard_map/reshape | solution.py:93
  236.4 9.4 %collective-permute-done.17 = bf16[1,256,1024]{2,1,0:T(8,128)(2,1)S(1)} collective-permute-done((bf16[1,256,1024]{2,1,0:T(8,128)(2,1)S(1)}, bf16[1,256,1024]{2,1,0:T(8,128)(2,1)S(1)}, u32[]{:S(2)}, u32[]{:S(2)}) %collective-permute-start.17) | collective-permute-done | bytes 524320 | tf_op jit(solution)/shard_map/ppermute | solution.py:107
  246.5 9.7 %collective-permute-done.18 = bf16[1,256,1024]{2,1,0:T(8,128)(2,1)S(1)} collective-permute-done((bf16[1,256,1024]{2,1,0:T(8,128)(2,1)S(1)}, bf16[1,256,1024]{2,1,0:T(8,128)(2,1)S(1)}, u32[]{:S(2)}, u32[]{:S(2)}) %collective-permute-start.18) | collective-permute-done | bytes 524320 | tf_op jit(solution)/shard_map/ppermute | solution.py:107
  256.3 23.9 %collective-permute-done.20 = bf16[1,256,1024]{2,1,0:T(8,128)(2,1)S(1)} collective-permute-done((bf16[1,256,1024]{2,1,0:T(8,128)(2,1)S(1)}, bf16[1,256,1024]{2,1,0:T(8,128)(2,1)S(1)}, u32[]{:S(2)}, u32[]{:S(2)}) %collective-permute-start.20) | collective-permute-done | bytes 524320 | tf_op jit(solution)/shard_map/ppermute | solution.py:107
  (180 shorter events, 59.5 us)
Async XLA Ops:
  0.0 27.8 %collective-permute-start.4 = (bf16[2048,256]{1,0:T(8,128)(2,1)}, bf16[2048,256]{1,0:T(8,128)(2,1)S(1)}, u32[]{:S(2)}, u32[]{:S(2)}) collective-permute-start(bf16[2048,256]{1,0:T(8,128)(2,1)} %param.7), channel_id=1, source_target_pairs={{0,3},{1,0},{2,1},{3,2},{4,7},{5,4},{6,5},{7,6},{8,11},{9,8},{10,9... | collective-permute-start | bytes 3145736 | tf_op jit(solution)/shard_map/ppermute | solution.py:12
  5.0 31.9 %collective-permute-start.7 = (s32[16,2]{0,1:T(2,128)}, s32[16,2]{0,1:T(2,128)S(1)}, u32[]{:S(2)}, u32[]{:S(2)}) collective-permute-start(s32[16,2]{0,1:T(2,128)} %param.8), channel_id=1, source_target_pairs={{0,3},{1,0},{2,1},{3,2},{4,7},{5,4},{6,5},{7,6},{8,11},{9,8},{10,9... | collective-permute-start | bytes 392 | tf_op jit(solution)/shard_map/ppermute | solution.py:12
  5.5 33.7 %collective-permute-start.10 = (bf16[128,1024]{1,0:T(8,128)(2,1)}, bf16[128,1024]{1,0:T(8,128)(2,1)S(1)}, u32[]{:S(2)}, u32[]{:S(2)}) collective-permute-start(bf16[128,1024]{1,0:T(8,128)(2,1)} %param.9), channel_id=1, source_target_pairs={{0,28},{4,0},{8,4},{12,8},{16,12},{20,16},{24,20},{28,24},{1,29},{... | collective-permute-start | bytes 786440 | tf_op jit(solution)/shard_map/ppermute | solution.py:12
  6.8 24.4 %collective-permute-start.13 = (s32[1,8]{1,0:T(1,128)}, s32[1,8]{1,0:T(1,128)S(1)}, u32[]{:S(2)}, u32[]{:S(2)}) collective-permute-start(s32[1,8]{1,0:T(1,128)} %param.10), channel_id=1, source_target_pairs={{0,28},{4,0},{8,4},{12,8},{16,12},{20,16},{24,20},{28,24},{1,29},{... | collective-permute-start | bytes 104 | tf_op jit(solution)/shard_map/ppermute | solution.py:12
  29.1 47.5 %collective-permute-start.5 = (bf16[2048,256]{1,0:T(8,128)(2,1)S(1)}, bf16[2048,256]{1,0:T(8,128)(2,1)S(1)}, u32[]{:S(2)}, u32[]{:S(2)}) collective-permute-start(bf16[2048,256]{1,0:T(8,128)(2,1)S(1)} %broadcast_select_fusion), channel_id=1, source_target_pairs={{0,2},{1,3},{2,0},{3,1},{4,6},{5,7},{6,4},{7,5},{8,10},{9,11},{10,... | collective-permute-start | bytes 3145736 | tf_op jit(solution)/shard_map/ppermute | solution.py:12
  35.4 45.3 %collective-permute-start.15 = (s32[1,8]{1,0:T(1,128)S(1)}, s32[1,8]{1,0:T(1,128)S(1)}, u32[]{:S(2)}, u32[]{:S(2)}) collective-permute-start(s32[1,8]{1,0:T(1,128)S(1)} %broadcast_select_fusion.6), channel_id=1, source_target_pairs={{0,16},{4,20},{8,24},{12,28},{16,0},{20,4},{24,8},{28,12},{1,17},{... | collective-permute-start | bytes 104 | tf_op jit(solution)/shard_map/ppermute | solution.py:12
  37.6 41.4 %collective-permute-start.8 = (s32[16,2]{0,1:T(2,128)S(1)}, s32[16,2]{0,1:T(2,128)S(1)}, u32[]{:S(2)}, u32[]{:S(2)}) collective-permute-start(s32[16,2]{0,1:T(2,128)S(1)} %broadcast_select_fusion.8), channel_id=1, source_target_pairs={{0,2},{1,3},{2,0},{3,1},{4,6},{5,7},{6,4},{7,5},{8,10},{9,11},{10,... | collective-permute-start | bytes 392 | tf_op jit(solution)/shard_map/ppermute | solution.py:12
  40.2 39.0 %collective-permute-start.11 = (bf16[128,1024]{1,0:T(8,128)(2,1)S(1)}, bf16[128,1024]{1,0:T(8,128)(2,1)S(1)}, u32[]{:S(2)}, u32[]{:S(2)}) collective-permute-start(bf16[128,1024]{1,0:T(8,128)(2,1)S(1)} %broadcast_select_fusion.2), channel_id=1, source_target_pairs={{0,24},{4,28},{8,0},{12,4},{16,8},{20,12},{24,16},{28,20},{1,25},{... | collective-permute-start | bytes 786440 | tf_op jit(solution)/shard_map/ppermute | solution.py:12
  76.7 25.0 %collective-permute-start.6 = (bf16[2048,256]{1,0:T(8,128)(2,1)S(1)}, bf16[2048,256]{1,0:T(8,128)(2,1)S(1)}, u32[]{:S(2)}, u32[]{:S(2)}) collective-permute-start(bf16[2048,256]{1,0:T(8,128)(2,1)S(1)} %broadcast_select_fusion.1), channel_id=1, source_target_pairs={{0,3},{1,0},{2,1},{3,2},{4,7},{5,4},{6,5},{7,6},{8,11},{9,8},{10,9... | collective-permute-start | bytes 3145736 | tf_op jit(solution)/shard_map/ppermute | solution.py:12
  79.1 22.6 %collective-permute-start.9 = (s32[16,2]{0,1:T(2,128)S(1)}, s32[16,2]{0,1:T(2,128)S(1)}, u32[]{:S(2)}, u32[]{:S(2)}) collective-permute-start(s32[16,2]{0,1:T(2,128)S(1)} %broadcast_select_fusion.9), channel_id=1, source_target_pairs={{0,3},{1,0},{2,1},{3,2},{4,7},{5,4},{6,5},{7,6},{8,11},{9,8},{10,9... | collective-permute-start | bytes 392 | tf_op jit(solution)/shard_map/ppermute | solution.py:12
  79.2 22.5 %collective-permute-start.12 = (bf16[128,1024]{1,0:T(8,128)(2,1)S(1)}, bf16[128,1024]{1,0:T(8,128)(2,1)S(1)}, u32[]{:S(2)}, u32[]{:S(2)}) collective-permute-start(bf16[128,1024]{1,0:T(8,128)(2,1)S(1)} %broadcast_select_fusion.3), channel_id=1, source_target_pairs={{0,16},{4,20},{8,24},{12,28},{16,0},{20,4},{24,8},{28,12},{1,17},{... | collective-permute-start | bytes 786440 | tf_op jit(solution)/shard_map/ppermute | solution.py:12
  102.2 14.9 %collective-permute-start = (bf16[2048,128]{1,0:T(8,128)(2,1)S(1)}, bf16[2048,128]{1,0:T(8,128)(2,1)S(1)}, u32[]{:S(2)}, u32[]{:S(2)}) collective-permute-start(bf16[2048,128]{1,0:T(8,128)(2,1)S(1)} %get-tuple-element.135), channel_id=1, source_target_pairs={{0,3},{1,0},{2,1},{3,2},{4,7},{5,4},{6,5},{7,6},{8,11},{9,8},{10,9... | collective-permute-start | bytes 1572872 | tf_op jit(solution)/shard_map/while/body/eval_jaxpr/ppermute | solution.py:12
  117.4 14.0 %collective-permute-start = (bf16[2048,128]{1,0:T(8,128)(2,1)S(1)}, bf16[2048,128]{1,0:T(8,128)(2,1)S(1)}, u32[]{:S(2)}, u32[]{:S(2)}) collective-permute-start(bf16[2048,128]{1,0:T(8,128)(2,1)S(1)} %get-tuple-element.135), channel_id=1, source_target_pairs={{0,3},{1,0},{2,1},{3,2},{4,7},{5,4},{6,5},{7,6},{8,11},{9,8},{10,9... | collective-permute-start | bytes 1572872 | tf_op jit(solution)/shard_map/while/body/eval_jaxpr/ppermute | solution.py:12
  131.6 13.9 %collective-permute-start = (bf16[2048,128]{1,0:T(8,128)(2,1)S(1)}, bf16[2048,128]{1,0:T(8,128)(2,1)S(1)}, u32[]{:S(2)}, u32[]{:S(2)}) collective-permute-start(bf16[2048,128]{1,0:T(8,128)(2,1)S(1)} %get-tuple-element.135), channel_id=1, source_target_pairs={{0,3},{1,0},{2,1},{3,2},{4,7},{5,4},{6,5},{7,6},{8,11},{9,8},{10,9... | collective-permute-start | bytes 1572872 | tf_op jit(solution)/shard_map/while/body/eval_jaxpr/ppermute | solution.py:12
  145.7 13.4 %collective-permute-start = (bf16[2048,128]{1,0:T(8,128)(2,1)S(1)}, bf16[2048,128]{1,0:T(8,128)(2,1)S(1)}, u32[]{:S(2)}, u32[]{:S(2)}) collective-permute-start(bf16[2048,128]{1,0:T(8,128)(2,1)S(1)} %get-tuple-element.135), channel_id=1, source_target_pairs={{0,3},{1,0},{2,1},{3,2},{4,7},{5,4},{6,5},{7,6},{8,11},{9,8},{10,9... | collective-permute-start | bytes 1572872 | tf_op jit(solution)/shard_map/while/body/eval_jaxpr/ppermute | solution.py:12
  159.4 12.9 %collective-permute-start = (bf16[2048,128]{1,0:T(8,128)(2,1)S(1)}, bf16[2048,128]{1,0:T(8,128)(2,1)S(1)}, u32[]{:S(2)}, u32[]{:S(2)}) collective-permute-start(bf16[2048,128]{1,0:T(8,128)(2,1)S(1)} %get-tuple-element.135), channel_id=1, source_target_pairs={{0,3},{1,0},{2,1},{3,2},{4,7},{5,4},{6,5},{7,6},{8,11},{9,8},{10,9... | collective-permute-start | bytes 1572872 | tf_op jit(solution)/shard_map/while/body/eval_jaxpr/ppermute | solution.py:12
  172.5 13.4 %collective-permute-start = (bf16[2048,128]{1,0:T(8,128)(2,1)S(1)}, bf16[2048,128]{1,0:T(8,128)(2,1)S(1)}, u32[]{:S(2)}, u32[]{:S(2)}) collective-permute-start(bf16[2048,128]{1,0:T(8,128)(2,1)S(1)} %get-tuple-element.135), channel_id=1, source_target_pairs={{0,3},{1,0},{2,1},{3,2},{4,7},{5,4},{6,5},{7,6},{8,11},{9,8},{10,9... | collective-permute-start | bytes 1572872 | tf_op jit(solution)/shard_map/while/body/eval_jaxpr/ppermute | solution.py:12
  186.1 12.9 %collective-permute-start = (bf16[2048,128]{1,0:T(8,128)(2,1)S(1)}, bf16[2048,128]{1,0:T(8,128)(2,1)S(1)}, u32[]{:S(2)}, u32[]{:S(2)}) collective-permute-start(bf16[2048,128]{1,0:T(8,128)(2,1)S(1)} %get-tuple-element.135), channel_id=1, source_target_pairs={{0,3},{1,0},{2,1},{3,2},{4,7},{5,4},{6,5},{7,6},{8,11},{9,8},{10,9... | collective-permute-start | bytes 1572872 | tf_op jit(solution)/shard_map/while/body/eval_jaxpr/ppermute | solution.py:12
  231.1 14.8 %collective-permute-start.17 = (bf16[1,256,1024]{2,1,0:T(8,128)(2,1)S(1)}, bf16[1,256,1024]{2,1,0:T(8,128)(2,1)S(1)}, u32[]{:S(2)}, u32[]{:S(2)}) collective-permute-start(bf16[1,256,1024]{2,1,0:T(8,128)(2,1)S(1)} %get-tuple-element.89), channel_id=1, source_target_pairs={{0,8},{4,12},{8,0},{12,4},{16,24},{20,28},{24,16},{28,20},{1,9},{5... | collective-permute-start | bytes 1572872 | tf_op jit(solution)/shard_map/ppermute | solution.py:107
  231.9 24.3 %collective-permute-start.18 = (bf16[1,256,1024]{2,1,0:T(8,128)(2,1)S(1)}, bf16[1,256,1024]{2,1,0:T(8,128)(2,1)S(1)}, u32[]{:S(2)}, u32[]{:S(2)}) collective-permute-start(bf16[1,256,1024]{2,1,0:T(8,128)(2,1)S(1)} %get-tuple-element.88), channel_id=1, source_target_pairs={{0,12},{4,8},{8,4},{12,0},{16,28},{20,24},{24,20},{28,16},{1,13},{... | collective-permute-start | bytes 1572872 | tf_op jit(solution)/shard_map/ppermute | solution.py:107
  232.9 23.3 %collective-permute-start.19 = (bf16[1,256,1024]{2,1,0:T(8,128)(2,1)S(1)}, bf16[1,256,1024]{2,1,0:T(8,128)(2,1)S(1)}, u32[]{:S(2)}, u32[]{:S(2)}) collective-permute-start(bf16[1,256,1024]{2,1,0:T(8,128)(2,1)S(1)} %get-tuple-element.87), channel_id=1, source_target_pairs={{0,16},{4,20},{8,24},{12,28},{16,0},{20,4},{24,8},{28,12},{1,17},{... | collective-permute-start | bytes 1572872 | tf_op jit(solution)/shard_map/ppermute | solution.py:107
  233.8 46.5 %collective-permute-start.20 = (bf16[1,256,1024]{2,1,0:T(8,128)(2,1)S(1)}, bf16[1,256,1024]{2,1,0:T(8,128)(2,1)S(1)}, u32[]{:S(2)}, u32[]{:S(2)}) collective-permute-start(bf16[1,256,1024]{2,1,0:T(8,128)(2,1)S(1)} %get-tuple-element.86), channel_id=1, source_target_pairs={{0,20},{4,16},{8,28},{12,24},{16,4},{20,0},{24,12},{28,8},{1,21},{... | collective-permute-start | bytes 1572872 | tf_op jit(solution)/shard_map/ppermute | solution.py:107
  234.6 45.7 %collective-permute-start.21 = (bf16[1,256,1024]{2,1,0:T(8,128)(2,1)S(1)}, bf16[1,256,1024]{2,1,0:T(8,128)(2,1)S(1)}, u32[]{:S(2)}, u32[]{:S(2)}) collective-permute-start(bf16[1,256,1024]{2,1,0:T(8,128)(2,1)S(1)} %get-tuple-element.85), channel_id=1, source_target_pairs={{0,24},{4,28},{8,16},{12,20},{16,8},{20,12},{24,0},{28,4},{1,25},{... | collective-permute-start | bytes 1572872 | tf_op jit(solution)/shard_map/ppermute | solution.py:107
  245.9 34.5 %collective-permute-start.22 = (bf16[1,256,1024]{2,1,0:T(8,128)(2,1)S(1)}, bf16[1,256,1024]{2,1,0:T(8,128)(2,1)S(1)}, u32[]{:S(2)}, u32[]{:S(2)}) collective-permute-start(bf16[1,256,1024]{2,1,0:T(8,128)(2,1)S(1)} %get-tuple-element.84), channel_id=1, source_target_pairs={{0,28},{4,24},{8,20},{12,16},{16,12},{20,8},{24,4},{28,0},{1,29},{... | collective-permute-start | bytes 1572872 | tf_op jit(solution)/shard_map/ppermute | solution.py:107
  (25 other events, 222.9 us)
